TPU v7x, 32 devices: a whole 2x2x4 slice. The times are simulated.
32 devices in a mesh: dp: 4 (over x, core), ctx: 8 (over z, y).
Axes of the slice: x: 2, y: 2, z: 4, core: 2. Of those that a mesh axis runs over, the one named last changes fastest.
Arguments:
- tokens: bfloat16 [4, 4096, 512], P('dp', 'ctx'), may hold values from -6 to 6
- piece_starts: int32 [4, 4], P('dp'), may hold values from 0 to 3840, as said below
- qkv_weight: bfloat16 [786432], P(('dp', 'ctx')), may hold values from -0.375 to 0.375
- out_weight: bfloat16 [262144], P(('dp', 'ctx')), may hold values from -0.75 to 0.75
- up_weight: bfloat16 [1048576], P(('dp', 'ctx')), may hold values from -0.25 to 0.25
- down_weight: bfloat16 [1048576], P(('dp', 'ctx')), may hold values from -0.125 to 0.125
- biases: bfloat16 [4096], P(('dp', 'ctx')), may hold values from -2 to 2
- norms: bfloat16 [2048], P(('dp', 'ctx'))
- cotangent: bfloat16 [4, 4096, 512], P('dp', 'ctx'), may hold values from -6 to 6
Outputs:
- output: bfloat16 [4, 4096, 512], P('dp', 'ctx')
- grad_tokens: float32 [4, 4096, 512], P('dp', 'ctx')
- grad_qkv: float32 [786432], P(('dp', 'ctx'))
- grad_out: float32 [262144], P(('dp', 'ctx'))
- grad_up: float32 [1048576], P(('dp', 'ctx'))
- grad_down: float32 [1048576], P(('dp', 'ctx'))
- grad_biases: float32 [4096], P(('dp', 'ctx'))
- grad_norms: float32 [2048], P(('dp', 'ctx'))
Inputs may be any that keep to these rules, and one draw needn't show every extreme that they name: `piece_starts`: each row holds 4 distinct multiples of 256 in increasing order; the first is 0 and the last 3840, so that every sequence opens and closes with a picture piece; a piece covers the 256 words from its start.
All inputs are finite; a program needn't handle non-finite values.
Results may differ from a plain program's by a relative error of at most 0.02.
Values may be sent and summed in bfloat16 or wider, within the bound.
A program may use at most 256 MiB of HBM per device.

v0:
```python
import jax
import jax.numpy as jnp
from jax import lax
from jax.sharding import PartitionSpec as P

HEADS = 8
PIECE = 256
eps_norm = 1e-05
masked_score = -1e30


def layer_norm(values, gain, shift):
    center = jnp.mean(values, axis=-1, keepdims=True)
    offsets = values - center
    spread = jnp.mean(offsets * offsets, axis=-1, keepdims=True)
    return offsets * lax.rsqrt(spread + eps_norm) * gain + shift


def gelu_exact(values):
    return jax.nn.gelu(values, approximate=False)


def piece_flags(positions, starts_row):
    opening = positions // PIECE * PIECE
    return jnp.any(opening[:, None] == starts_row[None, :], axis=1)


def visible(query_pos, query_flag, key_pos):
    causal = key_pos[None, :] <= query_pos[:, None]
    same_piece = key_pos[None, :] // PIECE == query_pos[:, None] // PIECE
    return jnp.logical_or(causal, jnp.logical_and(same_piece, query_flag[:, None]))


def to_blocks(arrays, shard_rows):
    block_len = 256
    block_count = shard_rows // block_len
    shaped = tuple((member.reshape(block_count, block_len, HEADS, -1) for member in arrays))
    return (block_len, block_count, shaped)


def keep_state(state):
    return state


def unpack(flats, model_width):
    qkv_flat, out_flat, up_flat, down_flat, bias_flat, norm_flat = flats
    hidden = up_flat.shape[0] // model_width
    return (
        qkv_flat.reshape(model_width, 3 * model_width),
        out_flat.reshape(model_width, model_width),
        up_flat.reshape(model_width, hidden),
        down_flat.reshape(hidden, model_width),
        bias_flat.astype(jnp.float32),
        norm_flat.astype(jnp.float32),
    )


def norm_back(values, gain, shift, upstream):
    _, pullback = jax.vjp(layer_norm, values, gain, shift)
    return pullback(upstream)


def column_sum(matrix):
    return jnp.sum(matrix.astype(jnp.float32), axis=0)


def query_terms(
    query_heads,
    grad_heads,
    own_lse,
    own_delta,
    query_pos,
    query_flag,
    key_block,
    value_block,
    key_pos,
    factor,
):
    scores = (
        jnp.einsum("qhd,khd->hqk", query_heads, key_block, preferred_element_type=jnp.float32)
        * factor
    )
    allowed = visible(query_pos, query_flag, key_pos)[None]
    softmax_p = jnp.where(allowed, jnp.exp(scores - own_lse[:, :, None]), 0.0)
    dprobs = jnp.einsum("qhd,khd->hqk", grad_heads, value_block, preferred_element_type=jnp.float32)
    dscores = (softmax_p * (dprobs - own_delta[:, :, None])).astype(jnp.bfloat16)
    return (
        jnp.einsum("hqk,khd->hqd", dscores, key_block, preferred_element_type=jnp.float32) * factor
    )


def key_terms(
    query_block,
    grad_block,
    lse_block,
    delta_block,
    remote_pos,
    remote_flag,
    key_heads,
    value_heads,
    key_pos,
    factor,
):
    scores = (
        jnp.einsum("qhd,khd->hqk", query_block, key_heads, preferred_element_type=jnp.float32)
        * factor
    )
    allowed = visible(remote_pos, remote_flag, key_pos)[None]
    softmax_p = jnp.where(allowed, jnp.exp(scores - lse_block[:, :, None]), 0.0)
    dprobs = jnp.einsum("qhd,khd->hqk", grad_block, value_heads, preferred_element_type=jnp.float32)
    dscores = (softmax_p * (dprobs - delta_block[:, :, None])).astype(jnp.bfloat16)
    grad_keys = (
        jnp.einsum("hqk,qhd->hkd", dscores, query_block, preferred_element_type=jnp.float32)
        * factor
    )
    grad_values = jnp.einsum(
        "hqk,qhd->hkd",
        softmax_p.astype(jnp.bfloat16),
        grad_block,
        preferred_element_type=jnp.float32,
    )
    return (grad_keys, grad_values)


def per_device(
    tokens, piece_starts, qkv_weight, out_weight, up_weight, down_weight, biases, norms, cotangent
):
    model_width = tokens.shape[2]
    seq_rows = tokens.shape[1]
    params = unpack(
        (
            lax.all_gather(qkv_weight, ("dp", "ctx"), axis=0, tiled=True),
            lax.all_gather(out_weight, ("dp", "ctx"), axis=0, tiled=True),
            lax.all_gather(up_weight, ("dp", "ctx"), axis=0, tiled=True),
            lax.all_gather(down_weight, ("dp", "ctx"), axis=0, tiled=True),
            lax.all_gather(biases, ("dp", "ctx"), axis=0, tiled=True),
            lax.all_gather(norms, ("dp", "ctx"), axis=0, tiled=True),
        ),
        model_width,
    )
    qkv_mat, out_mat, up_mat, down_mat, bias_all, norm_all = params
    hidden = up_mat.shape[1]
    head_dim = model_width // HEADS
    factor = head_dim ** (-0.5)
    first_row = lax.axis_index("ctx") * seq_rows
    last_row = first_row + seq_rows - 1
    query_pos = first_row + jnp.arange(seq_rows, dtype=jnp.int32)
    starts_row = piece_starts[0]
    query_flag = piece_flags(query_pos, starts_row)
    bias_q = bias_all[:model_width]
    bias_v = bias_all[model_width : 2 * model_width]
    bias_o = bias_all[2 * model_width : 3 * model_width]
    bias_up = bias_all[3 * model_width : 3 * model_width + hidden]
    bias_down = bias_all[3 * model_width + hidden :]
    gain_one = norm_all[:model_width]
    shift_one = norm_all[model_width : 2 * model_width]
    gain_two = norm_all[2 * model_width : 3 * model_width]
    shift_two = norm_all[3 * model_width :]
    inputs = tokens[0].astype(jnp.float32)
    first_in = layer_norm(inputs, gain_one, shift_one).astype(jnp.bfloat16)
    projected = jnp.dot(first_in, qkv_mat, preferred_element_type=jnp.float32)
    queries = (projected[:, :model_width] + bias_q).astype(jnp.bfloat16)
    key_rows = projected[:, model_width : 2 * model_width].astype(jnp.bfloat16)
    value_rows = (projected[:, 2 * model_width :] + bias_v).astype(jnp.bfloat16)
    query_heads = queries.reshape(seq_rows, HEADS, head_dim)
    key_heads = key_rows.reshape(seq_rows, HEADS, head_dim)
    value_heads = value_rows.reshape(seq_rows, HEADS, head_dim)
    start_state = (
        jnp.full((HEADS, seq_rows), masked_score, jnp.float32),
        jnp.zeros((HEADS, seq_rows), jnp.float32),
        jnp.zeros((HEADS, seq_rows, head_dim), jnp.float32),
    )
    shard = (
        lax.all_gather(key_rows, "ctx", axis=0, tiled=True),
        lax.all_gather(value_rows, "ctx", axis=0, tiled=True),
    )
    shard_rows = shard[0].shape[0]
    block_len, block_count, (key_blocks, value_blocks) = to_blocks(shard, shard_rows)

    def forward_one_block(state, block_in):
        running_max, running_sum, running_acc = state
        key_block, value_block, position = block_in
        key_pos = position * block_len + jnp.arange(block_len, dtype=jnp.int32)
        scores = (
            jnp.einsum("qhd,khd->hqk", query_heads, key_block, preferred_element_type=jnp.float32)
            * factor
        )
        allowed = visible(query_pos, query_flag, key_pos)[None]
        scores = jnp.where(allowed, scores, masked_score)
        new_max = jnp.maximum(running_max, jnp.max(scores, axis=-1))
        correction = jnp.exp(running_max - new_max)
        exp_scores = jnp.where(allowed, jnp.exp(scores - new_max[:, :, None]), 0.0)
        running_sum = running_sum * correction + jnp.sum(exp_scores, axis=-1)
        running_acc = running_acc * correction[:, :, None] + jnp.einsum(
            "hqk,khd->hqd",
            exp_scores.astype(jnp.bfloat16),
            value_block,
            preferred_element_type=jnp.float32,
        )
        return ((new_max, running_sum, running_acc), None)

    def forward_compute(state):
        return lax.scan(
            forward_one_block,
            state,
            (key_blocks, value_blocks, jnp.arange(block_count, dtype=jnp.int32)),
        )[0]

    run_max, run_sum, run_acc = lax.cond(
        jnp.int32(0) <= last_row, forward_compute, keep_state, start_state
    )
    mixed_heads = run_acc / run_sum[:, :, None]
    mixed_f = jnp.transpose(mixed_heads, (1, 0, 2)).reshape(seq_rows, model_width)
    mixed_b = mixed_f.astype(jnp.bfloat16)
    log_sum = run_max + jnp.log(run_sum)
    after_attn = inputs + jnp.dot(mixed_b, out_mat, preferred_element_type=jnp.float32) + bias_o
    second_in = layer_norm(after_attn, gain_two, shift_two).astype(jnp.bfloat16)
    pre_act = jnp.dot(second_in, up_mat, preferred_element_type=jnp.float32) + bias_up
    activated = gelu_exact(pre_act).astype(jnp.bfloat16)
    result = (
        after_attn + jnp.dot(activated, down_mat, preferred_element_type=jnp.float32) + bias_down
    )
    output = result.astype(jnp.bfloat16)[None]
    back = unpack(
        (
            lax.all_gather(qkv_weight, ("dp", "ctx"), axis=0, tiled=True),
            lax.all_gather(out_weight, ("dp", "ctx"), axis=0, tiled=True),
            lax.all_gather(up_weight, ("dp", "ctx"), axis=0, tiled=True),
            lax.all_gather(down_weight, ("dp", "ctx"), axis=0, tiled=True),
            lax.all_gather(biases, ("dp", "ctx"), axis=0, tiled=True),
            lax.all_gather(norms, ("dp", "ctx"), axis=0, tiled=True),
        ),
        model_width,
    )
    qkv_back, out_back, up_back, down_back, bias_back, norm_vec = back
    gain_one_b = norm_vec[:model_width]
    shift_one_b = norm_vec[model_width : 2 * model_width]
    gain_two_b = norm_vec[2 * model_width : 3 * model_width]
    shift_two_b = norm_vec[3 * model_width :]
    upstream = cotangent[0].astype(jnp.float32)
    grad_mlp = upstream.astype(jnp.bfloat16)
    grad_down_loc = jnp.einsum("ta,tb->ab", activated, grad_mlp, preferred_element_type=jnp.float32)
    grad_act = jnp.einsum("tb,ab->ta", grad_mlp, down_back, preferred_element_type=jnp.float32)
    _, gelu_pull = jax.vjp(gelu_exact, pre_act)
    grad_pre = gelu_pull(grad_act)[0].astype(jnp.bfloat16)
    grad_up_loc = jnp.einsum("ta,tb->ab", second_in, grad_pre, preferred_element_type=jnp.float32)
    grad_second = jnp.einsum("tb,ab->ta", grad_pre, up_back, preferred_element_type=jnp.float32)
    grad_after_part, grad_gain_two, grad_shift_two = norm_back(
        after_attn, gain_two_b, shift_two_b, grad_second
    )
    grad_after = upstream + grad_after_part
    grad_attn = grad_after.astype(jnp.bfloat16)
    grad_out_loc = jnp.einsum("ta,tb->ab", mixed_b, grad_attn, preferred_element_type=jnp.float32)
    grad_mixed = jnp.einsum(
        "tb,ab->ta", grad_attn, out_back, preferred_element_type=jnp.float32
    ).astype(jnp.bfloat16)
    grad_heads = grad_mixed.reshape(seq_rows, HEADS, head_dim)
    delta_rows = jnp.sum(
        grad_heads.astype(jnp.float32) * mixed_f.reshape(seq_rows, HEADS, head_dim), axis=-1
    )
    delta_heads = delta_rows.T
    stats = jnp.concatenate([log_sum.T, delta_rows], axis=1)
    all_stats = lax.all_gather(stats, "ctx", axis=0, tiled=True)
    zero_heads = jnp.zeros((HEADS, seq_rows, head_dim), jnp.float32)
    shard = (
        lax.all_gather(key_rows, "ctx", axis=0, tiled=True),
        lax.all_gather(value_rows, "ctx", axis=0, tiled=True),
    )
    shard_rows = shard[0].shape[0]
    query_block_len, query_block_count, (query_key_blocks, query_value_blocks) = to_blocks(
        shard, shard_rows
    )

    def query_one_block(total, block_in):
        key_block, value_block, position = block_in
        key_pos = position * query_block_len + jnp.arange(query_block_len, dtype=jnp.int32)
        term = query_terms(
            query_heads,
            grad_heads,
            log_sum,
            delta_heads,
            query_pos,
            query_flag,
            key_block,
            value_block,
            key_pos,
            factor,
        )
        return (total + term, None)

    def query_compute(total):
        return lax.scan(
            query_one_block,
            total,
            (query_key_blocks, query_value_blocks, jnp.arange(query_block_count, dtype=jnp.int32)),
        )[0]

    grad_q = lax.cond(jnp.int32(0) <= last_row, query_compute, keep_state, zero_heads)
    shard = (
        lax.all_gather(queries, "ctx", axis=0, tiled=True),
        lax.all_gather(grad_mixed, "ctx", axis=0, tiled=True),
    )
    shard_rows = shard[0].shape[0]
    key_block_len, key_block_count, (query_blocks, grad_blocks) = to_blocks(shard, shard_rows)

    def key_one_block(totals, block_in):
        query_block, grad_block, position = block_in
        begin = position * key_block_len
        remote_pos = begin + jnp.arange(key_block_len, dtype=jnp.int32)
        remote_flag = piece_flags(remote_pos, starts_row)
        stats_block = lax.dynamic_slice_in_dim(all_stats, begin, key_block_len, 0)
        lse_block = stats_block[:, :HEADS].T
        delta_block = stats_block[:, HEADS:].T
        grad_keys, grad_values = key_terms(
            query_block,
            grad_block,
            lse_block,
            delta_block,
            remote_pos,
            remote_flag,
            key_heads,
            value_heads,
            query_pos,
            factor,
        )
        return ((totals[0] + grad_keys, totals[1] + grad_values), None)

    def key_compute(totals):
        return lax.scan(
            key_one_block,
            totals,
            (query_blocks, grad_blocks, jnp.arange(key_block_count, dtype=jnp.int32)),
        )[0]

    grad_k, grad_v = lax.cond(
        jnp.int32(0) + shard_rows - 1 >= first_row,
        key_compute,
        keep_state,
        (zero_heads, zero_heads),
    )

    def merge_heads(grad_part):
        return (
            jnp.transpose(grad_part, (1, 0, 2)).reshape(seq_rows, model_width).astype(jnp.bfloat16)
        )

    grad_qkv_rows = jnp.concatenate(
        [merge_heads(grad_q), merge_heads(grad_k), merge_heads(grad_v)], axis=1
    )
    grad_qkv_loc = jnp.einsum(
        "ta,tb->ab", first_in, grad_qkv_rows, preferred_element_type=jnp.float32
    )
    grad_first = jnp.einsum(
        "tb,ab->ta", grad_qkv_rows, qkv_back, preferred_element_type=jnp.float32
    )
    grad_in_part, grad_gain_one, grad_shift_one = norm_back(
        inputs, gain_one_b, shift_one_b, grad_first
    )
    grad_tokens = (grad_after + grad_in_part)[None]
    grad_bias_loc = jnp.concatenate(
        [
            column_sum(grad_qkv_rows[:, :model_width]),
            column_sum(grad_qkv_rows[:, 2 * model_width :]),
            column_sum(grad_attn),
            column_sum(grad_pre),
            column_sum(grad_mlp),
        ]
    )
    grad_norm_loc = jnp.concatenate([grad_gain_one, grad_shift_one, grad_gain_two, grad_shift_two])
    summed = (
        lax.psum_scatter(grad_qkv_loc.reshape(-1), ("dp", "ctx"), scatter_dimension=0, tiled=True),
        lax.psum_scatter(grad_out_loc.reshape(-1), ("dp", "ctx"), scatter_dimension=0, tiled=True),
        lax.psum_scatter(grad_up_loc.reshape(-1), ("dp", "ctx"), scatter_dimension=0, tiled=True),
        lax.psum_scatter(grad_down_loc.reshape(-1), ("dp", "ctx"), scatter_dimension=0, tiled=True),
        lax.psum_scatter(grad_bias_loc, ("dp", "ctx"), scatter_dimension=0, tiled=True),
        lax.psum_scatter(grad_norm_loc, ("dp", "ctx"), scatter_dimension=0, tiled=True),
    )
    return (output, grad_tokens, summed[0], summed[1], summed[2], summed[3], summed[4], summed[5])


def solution(mesh):
    in_specs = (
        P("dp", "ctx", None),
        P("dp", None),
        P(("dp", "ctx")),
        P(("dp", "ctx")),
        P(("dp", "ctx")),
        P(("dp", "ctx")),
        P(("dp", "ctx")),
        P(("dp", "ctx")),
        P("dp", "ctx", None),
    )
    out_specs = (
        P("dp", "ctx", None),
        P("dp", "ctx", None),
        P(("dp", "ctx")),
        P(("dp", "ctx")),
        P(("dp", "ctx")),
        P(("dp", "ctx")),
        P(("dp", "ctx")),
        P(("dp", "ctx")),
    )
    return jax.shard_map(
        per_device, mesh=mesh, in_specs=in_specs, out_specs=out_specs, check_vma=False
    )
```

profile of v0, /device:TPU:0, one launch (start us, length us, event | category | flops | bytes accessed | tf_op | source)
XLA Modules:
  0.0 1414.8 jit_solution(3792771017945107225)
XLA Ops:
  11.6 42.1 %all-reduce = bf16[2048]{0:T(1024)(128)(2,1)S(1)} all-reduce(bf16[2048]{0:T(1024)(128)(2,1)S(1)} %dynamic-update-slice), channel_id=1, replica_groups=mesh['dp'=4,'ctx'=8] {'dp','ctx'}, use_global_device_ids=true, to_apply=%add | all-reduce | flops 2048 | bytes 8192
  53.7 65.8 %all-gather = bf16[32,1,128]{2,1,0:T(2,128)(2,1)S(1)} all-gather(bf16[1,1,128]{2,1,0:T(2,128)(2,1)} %bitcast.300), channel_id=1, replica_groups=mesh['dp'=4,'ctx'=8] {'dp','ctx'}, dimensions={0}, use_global_device_ids=true | all-gather | bytes 8448 | tf_op jit(solution)/shard_map/all_gather | solution.py:136
  131.3 67.8 %all_gather.45 = bf16[262144]{0:T(1024)(128)(2,1)S(1)} all-gather(bf16[8192]{0:T(1024)(128)(2,1)S(1)} %copy-done.33), channel_id=1, replica_groups=mesh['dp'=4,'ctx'=8] {'dp','ctx'}, dimensions={0}, use_global_device_ids=true | all-gather | bytes 540672 | tf_op jit(solution)/shard_map/all_gather | solution.py:133
  210.1 50.6 %all-gather.13.cloned.1.call-done = bf16[4096,512]{1,0:T(8,128)(2,1)} async-done(((bf16[512,512]{1,0:T(8,128)(2,1)}), bf16[4096,512]{1,0:T(8,128)(2,1)}) %all-gather.13.cloned.1.call-update) | async-done | bytes 4194320 | tf_op jit(solution)/shard_map/all_gather | solution.py:175
  260.7 6.4 copy.89
  267.1 5.8 copy.112
  272.9 62.1 %all-gather.11.cloned.1.call-done = bf16[4096,512]{1,0:T(8,128)(2,1)} async-done(((bf16[512,512]{1,0:T(8,128)(2,1)}), bf16[4096,512]{1,0:T(8,128)(2,1)}) %all-gather.11.cloned.1.call-update) | async-done | bytes 4194320 | tf_op jit(solution)/shard_map/all_gather | solution.py:174
  334.9 6.4 copy.87
  347.4 248.7 %conditional.3 = (f32[8,512]{1,0:T(8,128)}, f32[8,512]{1,0:T(8,128)}, f32[8,512,64]{1,2,0:T(8,128)}, f32[8,512]{1,0:T(8,128)S(1)}) conditional(s32[]{:T(128)} %convert_element_type.146, () %tuple.77, (s32[512]{0:T(512)S(1)}, pred[512]{0:T(512)(128)(4,1)S(1)}, bf16[16,256,8,64]{1,0,3,2:T(8,128)(2,1)S(1)}, bf16[512,8,64]{0,2,1:T(8,128)(2,1)S(1)}, ...), branch_computations={%region_3.4_spmd, %region_4.9_spmd} | conditional | flops 283409920 | bytes 50127792 | solution.py:209
  354.3 241.1 %while.45 = (s32[]{:T(128)}, f32[8,512]{1,0:T(8,128)}, f32[8,512]{1,0:T(8,128)}, f32[8,512,64]{1,2,0:T(8,128)}, s32[16]{0:T(128)S(1)}, /*index=5*/s32[512]{0:T(5...) while((s32[]{:T(128)}, f32[8,512]{1,0:T(8,128)}, ...), condition=%wide.region_8.8_spmd.clone, body=%wide.region_5.7_spmd.clone.sunk | while | flops 283408896 | bytes 33311440 | solution.py:203
  599.4 11.5 multiply_convert_fusion.1
  641.5 181.9 %conditional.4 = (f32[8,512,64]{1,2,0:T(8,128)}) conditional(s32[]{:T(128)} %convert_element_type.146, () %tuple.79, (s32[512]{0:T(512)S(1)}, pred[512]{0:T(512)(128)(4,1)S(1)}, bf16[16,256,8,64]{1,0,3,2:T(8,128)(2,1)}, bf16[512,8,64]{0,2,1:T(8,128)(2,1)S(1)}, f32[8,512]{1,0:T(8,128)S(1)}, /*index=5*/bf16[16,256,8,64]{1,0,3,2:T(8,128)(2,1)}, ...), branch_computations={%region_14.15_spmd, %region_15.18_spmd} | conditional | flops 410267136 | bytes 46196136 | solution.py:298
  641.5 5.8 copy.95
  650.7 172.7 %while.46 = (s32[]{:T(128)}, f32[8,512,64]{1,2,0:T(8,128)}, s32[16]{0:T(128)S(1)}, s32[512]{0:T(512)S(1)}, s32[512,1]{0,1:T(1,128)S(1)}, /*index=5*/s32[512,1]{0...) while((s32[]{:T(128)}, f32[8,512,64]{1,2,0:T(8,128)}, ...), condition=%wide.region_17.17_spmd.clone, body=%wide.region_16.16_spmd.clone.sunk | while | flops 410266112 | bytes 12635323 | solution.py:292
  823.4 30.9 %all_gather.50 = f32[4096,16]{0,1:T(8,128)S(1)} all-gather(f32[512,16]{0,1:T(8,128)S(1)} %pad_maximum_fusion.3), channel_id=1, replica_groups=mesh['dp'=4,'ctx'=8] {'ctx'}, dimensions={0}, use_global_device_ids=true | all-gather | bytes 294912 | tf_op jit(solution)/shard_map/all_gather | solution.py:263
  857.0 304.2 %conditional.5 = (f32[8,512,64]{1,2,0:T(8,128)}, bf16[8,512,64]{1,2,0:T(8,128)(2,1)}, f32[512]{0:T(512)S(1)}) conditional(s32[]{:T(128)} %convert_element_type.166, () %tuple.81, (bf16[4096,512]{1,0:T(8,128)(2,1)}, bf16[4096,512]{0,1:T(8,128)(2,1)}, bf16[512,512]{1,0:T(8,128)(2,1)}, bf16[512,512]{1,0:T(8,128)(2,1)}, s32[512]{0:T(512)S(1)}, ...), branch_computations={%region_18.19_spmd, %region_19.23_spmd} | conditional | flops 549995520 | bytes 56584196 | solution.py:335
  857.6 11.2 reshape.730
  868.8 9.1 copy.84
  888.9 271.4 %while.47 = (s32[]{:T(128)}, f32[8,512,64]{1,2,0:T(8,128)}, f32[8,512,64]{1,2,0:T(8,128)S(1)}, s32[512]{0:T(512)S(1)}, s32[16]{0:T(128)}, /*index=5*/s32[1,512]{...) while((s32[]{:T(128)}, f32[8,512,64]{1,2,0:T(8,128)}, ...), condition=%wide.region_22.22_spmd.clone, body=%wide.region_20.21_spmd.clone.sunk | while | flops 549208576 | bytes 19347220 | solution.py:329
  916.8 5.7 fusion.196
  933.8 5.7 fusion.196
  950.8 5.7 fusion.196
  984.7 5.7 fusion.196
  1018.7 5.7 fusion.196
  1052.7 5.7 fusion.196
  1069.6 5.7 fusion.196
  1086.6 5.7 fusion.196
  1120.6 5.7 fusion.196
  1137.6 5.7 fusion.196
  1154.6 5.7 fusion.196
  1186.7 38.7 %all-reduce.7 = (f32[4096]{0:T(1024)S(1)}, f32[2048]{0:T(1024)S(1)}) all-reduce(f32[4096]{0:T(1024)S(1)} %constant_dynamic-update-slice_fusion, f32[2048]{0:T(1024)S(1)} %pad_maximum_fusion.4), channel_id=6, replica_groups=mesh['dp'=4,'ctx'=8] {'dp','ctx'}, use_global_device_ids=true, to_apply=%region_34.35.clone | all-reduce | flops 6144 | bytes 49152
  1226.6 175.1 %all-reduce.11.cloned.1.call-done = (f32[786432]{0:T(1024)}, f32[262144]{0:T(1024)}, f32[1048576]{0:T(1024)}, f32[1048576]{0:T(1024)}) async-done(((f32[786432]{0:T(1024)}, f32[262144]{0:T(1024)}, f32[1048576]{0:T(1024)}, f32[1048576]{0:T(1024)}), (f32[786432]{0:T(1024)}, f32[262144]{0:T(1024)}, f32[1048576]{0:T(1024)}, f32[1048576]{0:T(1024)})) %all-reduce.11.cloned.1.call-update) | async-done | bytes 12582928
  (685 shorter events, 714.7 us)
Async XLA Ops:
  7.2 113.8 %all-gather.9.cloned.1.call-start = ((), (), s32[]{:S(2)}) async-start(), calls=%async_computation | async-start | bytes 1622016 | tf_op jit(solution)/shard_map/all_gather | solution.py:132
  7.9 193.6 %all-gather.15.cloned.1.call-start = ((), (), s32[]{:S(2)}) async-start(), calls=%async_computation.3 | async-start | bytes 2162688 | tf_op jit(solution)/shard_map/all_gather | solution.py:134
  8.7 197.1 %all-gather.17.cloned.1.call-start = ((), (), s32[]{:S(2)}) async-start(), calls=%async_computation.4 | async-start | bytes 2162688 | tf_op jit(solution)/shard_map/all_gather | solution.py:135
  9.4 251.3 %all-gather.13.cloned.1.call-start = ((), (), s32[]{:S(2)}) async-start(), calls=%async_computation.2 | async-start | bytes 4718592 | tf_op jit(solution)/shard_map/all_gather | solution.py:175
  125.4 5.9 copy-start.33
  125.4 74.8 %copy-start.19 = (bf16[1,512,512]{2,1,0:T(8,128)(2,1)S(1)}, bf16[1,512,512]{2,1,0:T(8,128)(2,1)}, u32[]{:S(2)}) copy-start(bf16[1,512,512]{2,1,0:T(8,128)(2,1)} %param.29) | copy-start | bytes 1572868
  128.4 72.8 %copy-start.9 = (bf16[512,512]{1,0:T(8,128)(2,1)S(1)}, bf16[512,512]{1,0:T(8,128)(2,1)}, u32[]{:S(2)}) copy-start(bf16[512,512]{1,0:T(8,128)(2,1)} %get-tuple-element.1027) | copy-start | bytes 1572868
  128.4 206.5 %all-gather.11.cloned.1.call-start = ((), (), s32[]{:S(2)}) async-start(), calls=%async_computation.1 | async-start | bytes 4718592 | tf_op jit(solution)/shard_map/all_gather | solution.py:174
  130.6 726.4 %all-gather.19.cloned.1.call-start = ((), (), s32[]{:S(2)}) async-start(), calls=%async_computation.5 | async-start | bytes 4718592 | tf_op jit(solution)/shard_map/all_gather | solution.py:300
  131.2 725.8 %all-gather.21.cloned.1.call-start = ((), (), s32[]{:S(2)}) async-start(), calls=%async_computation.6 | async-start | bytes 4718592 | tf_op jit(solution)/shard_map/all_gather | solution.py:301
  200.4 423.5 %copy-start.6 = (bf16[1,512,512]{1,2,0:T(8,128)(2,1)}, bf16[1,512,512]{1,2,0:T(8,128)(2,1)S(1)}, u32[]{:S(2)}) copy-start(bf16[1,512,512]{1,2,0:T(8,128)(2,1)S(1)} %copy.93) | copy-start | bytes 1572868
  372.7 5.7 copy-start
  388.0 5.7 copy-start
  403.2 5.6 copy-start
  418.4 5.6 copy-start
  433.5 5.6 copy-start
  448.7 5.6 copy-start
  463.9 5.6 copy-start
  479.1 5.6 copy-start
  494.2 5.6 copy-start
  509.4 5.6 copy-start
  524.6 5.6 copy-start
  539.8 5.6 copy-start
  554.9 5.6 copy-start
  570.1 5.6 copy-start
  585.3 5.6 copy-start
  599.4 11.6 copy-start.13
  599.4 11.6 copy-start.20
  624.0 7.5 copy-start.30
  628.4 773.2 %all-reduce.11.cloned.1.call-start = ((), (), s32[]{:S(2)}) async-start(), calls=%async_computation.7 | async-start | bytes 25165824
  641.5 5.8 copy-start.2
  1176.4 5.6 copy-start.27
  (34 other events, 117.9 us)
Sparse Core Ops, SparseCore 0:
  10.9 57.8 all-gather.8
  71.7 55.3 all-gather.14
  130.2 56.0 all-gather.16
  188.3 72.3 all-gather.12
  263.2 71.6 all-gather.10
  336.9 71.6 all-gather.18
  628.6 73.0 all-gather.20
  1171.2 230.4 all-reduce.10
where the time goes:
time: 1430 us; the launch traced here: 1410 us
  matrix products  510 us (36%)
  waiting for transfers between devices  290 us (20%)
  blocking collectives  245 us (17%)
  local copies, waits for them, and re-layouts  180 us (13%)
  other arithmetic  141 us (10%)
  loops' own time  33 us (2%)
  between operations  15 us (1%)
    unnamed x9, waiting for transfers between devices  178 us
    dot_general x16, matrix products, key_terms(): jnp.einsum('hqk,qhd->hkd', dscores, query_block, preferred_element_type=j...  91 us
    dot_general x16, matrix products, query_terms(): jnp.einsum('hqk,khd->hqd', dscores, key_block, preferred_element_type=jnp...  88 us
    unnamed x2, blocking collectives  80.8 us
    all_gather x1, blocking collectives, per_device(): lax.all_gather(out_weight, ('dp', 'ctx'), axis=0, tiled=True)  67.8 us
    all_gather x1, blocking collectives, per_device(): lax.all_gather(biases, ('dp', 'ctx'), axis=0, tiled=True)  65.8 us
    all_gather x1, waiting for transfers between devices, per_device(): lax.all_gather(key_rows, 'ctx', axis=0, tiled=True)  62.1 us
    dot_general x16, matrix products, query_terms(): jnp.einsum('qhd,khd->hqk', query_heads, key_block, preferred_element_type...  60.4 us
  transfers between devices with their start and end apart: 8, of which 3 were waited for; matrix products, arithmetic and copies ran while one was open for 36% of the time, Pallas kernels for 0%

commit v1 on v0

--- a/solution.py
+++ b/solution.py
@@ -125,6 +125,32 @@
 def per_device(
     tokens, piece_starts, qkv_weight, out_weight, up_weight, down_weight, biases, norms, cotangent
 ):
+
+    def launch_sector(xx):
+        ax_name = "ctx"
+        after, v_now, all_rows = (
+            lax.psum(1, axis_name=ax_name),
+            lax.axis_index(ax_name),
+            xx.shape[0],
+        )
+        panels = [(u, (u + 1) % after) for u in range(after)]
+        heap = [(u, (u - 1) % after) for u in range(after)]
+        clean = jnp.zeros((*xx.shape[:0], after * all_rows, *xx.shape[1:]), xx.dtype)
+        clean = lax.dynamic_update_slice_in_dim(clean, xx, v_now * all_rows, axis=0)
+        state_next = newest = xx
+        long_array = after // 2
+        for num in range(1, long_array + 1):
+            state_next = lax.ppermute(state_next, axis_name=ax_name, perm=panels)
+            clean = lax.dynamic_update_slice_in_dim(
+                clean, state_next, (v_now - num) % after * all_rows, axis=0
+            )
+            if num < after - long_array:
+                newest = lax.ppermute(newest, perm=heap, axis_name=ax_name)
+                clean = lax.dynamic_update_slice_in_dim(
+                    clean, newest, (v_now + num) % after * all_rows, axis=0
+                )
+        return clean
+
     model_width = tokens.shape[2]
     seq_rows = tokens.shape[1]
     params = unpack(
@@ -170,10 +196,7 @@
         jnp.zeros((HEADS, seq_rows), jnp.float32),
         jnp.zeros((HEADS, seq_rows, head_dim), jnp.float32),
     )
-    shard = (
-        lax.all_gather(key_rows, "ctx", axis=0, tiled=True),
-        lax.all_gather(value_rows, "ctx", axis=0, tiled=True),
-    )
+    shard = (launch_sector(key_rows), lax.all_gather(value_rows, "ctx", axis=0, tiled=True))
     shard_rows = shard[0].shape[0]
     block_len, block_count, (key_blocks, value_blocks) = to_blocks(shard, shard_rows)
 

time: 1430 us -> 1430 us (level)
  waiting for transfers between devices: 290 us -> 234 us
  local copies, waits for them, and re-layouts: 180 us -> 211 us
  starting transfers between devices: 0.31 us -> 17.1 us
    all_gather x1, waiting for transfers between devices: 62.1 us -> 0.01 us  [per_device(): lax.all_gather(key_rows, 'ctx', axis=0, tiled=True)]
    ppermute x0 -> x7, waiting for transfers between devices: none -> 56.1 us  [the longest x4 56 us: launch_sector(): state_next = lax.ppermute(state_next, axis_name=ax_name, perm=panels)]
    all_gather x1, waiting for transfers between devices: 50.6 us -> 0.01 us  [per_device(): lax.all_gather(value_rows, 'ctx', axis=0, tiled=True)]
    ppermute x0 -> x7, starting transfers between devices: none -> 16.7 us  [the longest x3 9.24 us: launch_sector(): newest = lax.ppermute(newest, perm=heap, axis_name=ax_name)]
    cond x5 -> x10, local copies, waits for them, and re-layouts: 16.2 us -> 32.3 us
    unnamed x103 -> x104, local copies, waits for them, and re-layouts: 36.4 us -> 31.3 us
  transfers between devices with their start and end apart: 8 -> 15, of which waited for: 3 -> 5; matrix products, arithmetic and copies ran while one was open for 36% -> 39% of each run, Pallas kernels for 0% -> 0%
where the time goes in v1:
time: 1430 us; the launch traced here: 1420 us
  matrix products  511 us (36%)
  blocking collectives  256 us (18%)
  waiting for transfers between devices  234 us (16%)
  local copies, waits for them, and re-layouts  211 us (15%)
  other arithmetic  140 us (10%)
  loops' own time  33.6 us (2%)
  starting transfers between devices  17.1 us (1%)
  between operations  15 us (1%)
    unnamed x9, waiting for transfers between devices  178 us
    dot_general x16, matrix products, key_terms(): jnp.einsum('hqk,qhd->hkd', dscores, query_block, preferred_element_type=j...  91.1 us
    dot_general x16, matrix products, query_terms(): jnp.einsum('hqk,khd->hqd', dscores, key_block, preferred_element_type=jnp...  89.9 us
    unnamed x2, blocking collectives  81.2 us
    all_gather x1, blocking collectives, per_device(): lax.all_gather(out_weight, ('dp', 'ctx'), axis=0, tiled=True)  78.6 us
    all_gather x1, blocking collectives, per_device(): lax.all_gather(biases, ('dp', 'ctx'), axis=0, tiled=True)  65.8 us
    dot_general x16, matrix products, forward_one_block(): jnp.einsum('qhd,khd->hqk', query_heads, key_block, preferred_element_type...  61 us
    dot_general x16, matrix products, query_terms(): jnp.einsum('qhd,khd->hqk', query_heads, key_block, preferred_element_type...  59.8 us
  transfers between devices with their start and end apart: 15, of which 5 were waited for; matrix products, arithmetic and copies ran while one was open for 39% of the time, Pallas kernels for 0%

profile of v1, /device:TPU:0, one launch (start us, length us, event | category | flops | bytes accessed | tf_op | source)
XLA Modules:
  0.0 1419.4 jit_solution(5526134584638196509)
XLA Ops:
  11.6 42.1 %all-reduce = bf16[2048]{0:T(1024)(128)(2,1)S(1)} all-reduce(bf16[2048]{0:T(1024)(128)(2,1)S(1)} %dynamic-update-slice), channel_id=1, replica_groups=mesh['dp'=4,'ctx'=8] {'dp','ctx'}, use_global_device_ids=true, to_apply=%add | all-reduce | flops 2048 | bytes 8192
  53.7 65.8 %all-gather = bf16[32,1,128]{2,1,0:T(2,128)(2,1)S(1)} all-gather(bf16[1,1,128]{2,1,0:T(2,128)(2,1)} %bitcast.301), channel_id=1, replica_groups=mesh['dp'=4,'ctx'=8] {'dp','ctx'}, dimensions={0}, use_global_device_ids=true | all-gather | bytes 8448 | tf_op jit(solution)/shard_map/all_gather | solution.py:162
  135.4 12.9 collective-permute-done
  153.1 20.3 %collective-permute-done.2 = bf16[512,512]{1,0:T(8,128)(2,1)S(1)} collective-permute-done((bf16[512,512]{1,0:T(8,128)(2,1)S(1)}, bf16[512,512]{1,0:T(8,128)(2,1)S(1)}, u32[]{:S(2)}, u32[]{:S(2)}) %collective-permute-start.2) | collective-permute-done | bytes 524320 | tf_op jit(solution)/shard_map/ppermute | solution.py:143
  178.2 22.8 %collective-permute-done.4 = bf16[512,512]{1,0:T(8,128)(2,1)} collective-permute-done((bf16[512,512]{1,0:T(8,128)(2,1)S(1)}, bf16[512,512]{1,0:T(8,128)(2,1)}, u32[]{:S(2)}, u32[]{:S(2)}) %collective-permute-start.4) | collective-permute-done | bytes 524320 | tf_op jit(solution)/shard_map/ppermute | solution.py:143
  203.6 78.6 %all_gather.43 = bf16[262144]{0:T(1024)(128)(2,1)S(1)} all-gather(bf16[8192]{0:T(1024)(128)(2,1)S(1)} %copy-done.35), channel_id=1, replica_groups=mesh['dp'=4,'ctx'=8] {'dp','ctx'}, dimensions={0}, use_global_device_ids=true | all-gather | bytes 540672 | tf_op jit(solution)/shard_map/all_gather | solution.py:159
  293.9 6.6 copy.104
  306.2 276.0 %conditional.3 = (f32[8,512]{1,0:T(8,128)}, f32[8,512]{1,0:T(8,128)}, f32[8,512,64]{1,2,0:T(8,128)}, f32[8,512]{1,0:T(8,128)S(1)}) conditional(s32[]{:T(128)} %convert_element_type.146, () %tuple.143, (s32[]{:T(128)}, bf16[512,512]{1,0:T(8,128)(2,1)S(1)}, s32[]{:T(128)}, s32[]{:T(128)}, bf16[512,512]{1,0:T(8,128)(2,1)S(1)}, ...), branch_computations={%region_3.4_spmd, %region_4.9_spmd.clone.clone} | conditional | flops 283410048 | bytes 96266384 | solution.py:232
  337.9 243.5 %while.59 = (s32[]{:T(128)}, f32[8,512]{1,0:T(8,128)}, f32[8,512]{1,0:T(8,128)}, f32[8,512,64]{1,2,0:T(8,128)}, s32[16]{0:T(128)S(1)}, /*index=5*/s32[512]{0:T(5...) while((s32[]{:T(128)}, f32[8,512]{1,0:T(8,128)}, ...), condition=%wide.region_8.8_spmd.clone, body=%wide.region_5.7_spmd.clone.sunk | while | flops 283408896 | bytes 33311440 | solution.py:226
  585.5 11.6 multiply_convert_fusion.1
  627.6 199.8 %conditional.4 = (f32[8,512,64]{1,2,0:T(8,128)}) conditional(s32[]{:T(128)} %convert_element_type.146, () %tuple.145, (bf16[4096,512]{1,0:T(8,128)(2,1)}, s32[512]{0:T(512)S(1)}, pred[512]{0:T(512)(128)(4,1)S(1)}, bf16[512,8,64]{0,2,1:T(8,128)(2,1)S(1)}, f32[8,512]{1,0:T(8,128)S(1)}, /*index=5*/bf16[16,256,8,64]{1,0,3,2:T(8,128)(2,1)}, ...), branch_computations={%region_14.15_spmd, %region_15.18_spmd} | conditional | flops 410267136 | bytes 37807500 | solution.py:321
  627.6 11.2 reshape.742
  638.9 9.1 copy.97
  648.0 5.7 copy.118
  653.7 173.7 %while.60 = (s32[]{:T(128)}, f32[8,512,64]{1,2,0:T(8,128)}, s32[16]{0:T(128)S(1)}, s32[512]{0:T(512)S(1)}, s32[512,1]{0,1:T(1,128)S(1)}, /*index=5*/s32[512,1]{0...) while((s32[]{:T(128)}, f32[8,512,64]{1,2,0:T(8,128)}, ...), condition=%wide.region_17.17_spmd.clone, body=%wide.region_16.16_spmd.clone.sunk | while | flops 410266112 | bytes 12635323 | solution.py:315
  827.4 30.8 %all_gather.49 = f32[4096,16]{0,1:T(8,128)S(1)} all-gather(f32[512,16]{0,1:T(8,128)S(1)} %pad_maximum_fusion.3), channel_id=1, replica_groups=mesh['dp'=4,'ctx'=8] {'ctx'}, dimensions={0}, use_global_device_ids=true | all-gather | bytes 294912 | tf_op jit(solution)/shard_map/all_gather | solution.py:286
  861.0 303.2 %conditional.5 = (f32[8,512,64]{1,2,0:T(8,128)}, bf16[8,512,64]{1,2,0:T(8,128)(2,1)}, f32[512]{0:T(512)S(1)}) conditional(s32[]{:T(128)} %convert_element_type.166, () %tuple.147, (bf16[4096,512]{1,0:T(8,128)(2,1)}, bf16[4096,512]{0,1:T(8,128)(2,1)}, bf16[512,512]{1,0:T(8,128)(2,1)S(1)}, bf16[512,512]{1,0:T(8,128)(2,1)}, s32[512]{0:T(512)S(1)}, ...), branch_computations={%region_18.19_spmd, %region_19.23_spmd} | conditional | flops 549995520 | bytes 58681376 | solution.py:358
  861.6 11.4 reshape.743
  873.0 9.1 copy.98
  893.0 270.3 %while.61 = (s32[]{:T(128)}, f32[8,512,64]{1,2,0:T(8,128)}, f32[8,512,64]{1,2,0:T(8,128)S(1)}, s32[512]{0:T(512)S(1)}, s32[16]{0:T(128)}, /*index=5*/s32[1,512]{...) while((s32[]{:T(128)}, f32[8,512,64]{1,2,0:T(8,128)}, ...), condition=%wide.region_22.22_spmd.clone, body=%wide.region_20.21_spmd.clone.sunk | while | flops 549208576 | bytes 19347220 | solution.py:352
  920.8 5.7 fusion.196
  937.7 5.7 fusion.196
  954.6 5.7 fusion.196
  971.5 5.7 fusion.196
  988.4 5.7 fusion.196
  1022.2 5.7 fusion.196
  1056.1 5.7 fusion.196
  1089.9 5.7 fusion.196
  1123.7 5.7 fusion.196
  1157.6 5.7 fusion.196
  1189.7 39.1 %all-reduce.7 = (f32[4096]{0:T(1024)S(1)}, f32[2048]{0:T(1024)S(1)}) all-reduce(f32[4096]{0:T(1024)S(1)} %constant_dynamic-update-slice_fusion.7, f32[2048]{0:T(1024)S(1)} %pad_maximum_fusion.4), channel_id=6, replica_groups=mesh['dp'=4,'ctx'=8] {'dp','ctx'}, use_global_device_ids=true, to_apply=%region_34.35.clone | all-reduce | flops 6144 | bytes 49152
  1230.0 176.2 %all-reduce.11.cloned.1.call-done = (f32[786432]{0:T(1024)}, f32[262144]{0:T(1024)}, f32[1048576]{0:T(1024)}, f32[1048576]{0:T(1024)}) async-done(((f32[786432]{0:T(1024)}, f32[262144]{0:T(1024)}, f32[1048576]{0:T(1024)}, f32[1048576]{0:T(1024)}), (f32[786432]{0:T(1024)}, f32[262144]{0:T(1024)}, f32[1048576]{0:T(1024)}, f32[1048576]{0:T(1024)})) %all-reduce.11.cloned.1.call-update) | async-done | bytes 12582928
  (720 shorter events, 760.3 us)
Async XLA Ops:
  7.2 113.8 %all-gather.9.cloned.1.call-start = ((), (), s32[]{:S(2)}) async-start(), calls=%async_computation | async-start | bytes 1622016 | tf_op jit(solution)/shard_map/all_gather | solution.py:158
  7.9 277.4 %all-gather.13.cloned.1.call-start = ((), (), s32[]{:S(2)}) async-start(), calls=%async_computation.2 | async-start | bytes 2162688 | tf_op jit(solution)/shard_map/all_gather | solution.py:160
  8.7 280.9 %all-gather.15.cloned.1.call-start = ((), (), s32[]{:S(2)}) async-start(), calls=%async_computation.3 | async-start | bytes 2162688 | tf_op jit(solution)/shard_map/all_gather | solution.py:161
  9.4 284.5 %all-gather.11.cloned.1.call-start = ((), (), s32[]{:S(2)}) async-start(), calls=%async_computation.1 | async-start | bytes 4718592 | tf_op jit(solution)/shard_map/all_gather | solution.py:199
  119.5 5.8 copy-start.24
  125.4 78.2 %copy-start.35 = (bf16[8192]{0:T(1024)(128)(2,1)S(1)}, bf16[8192]{0:T(1024)(128)(2,1)}, u32[]{:S(2)}) copy-start(bf16[8192]{0:T(1024)(128)(2,1)} %param.24) | copy-start | bytes 49156
  125.4 157.9 %copy-start.18 = (bf16[1,512,512]{2,1,0:T(8,128)(2,1)S(1)}, bf16[1,512,512]{2,1,0:T(8,128)(2,1)}, u32[]{:S(2)}) copy-start(bf16[1,512,512]{2,1,0:T(8,128)(2,1)} %param.29) | copy-start | bytes 1572868
  128.4 156.7 %copy-start.9 = (bf16[512,512]{1,0:T(8,128)(2,1)S(1)}, bf16[512,512]{1,0:T(8,128)(2,1)}, u32[]{:S(2)}) copy-start(bf16[512,512]{1,0:T(8,128)(2,1)} %get-tuple-element.1944) | copy-start | bytes 1572868
  128.4 499.2 %all-gather.17.cloned.1.call-start = ((), (), s32[]{:S(2)}) async-start(), calls=%async_computation.4 | async-start | bytes 4718592 | tf_op jit(solution)/shard_map/all_gather | solution.py:289
  130.6 730.3 %all-gather.19.cloned.1.call-start = ((), (), s32[]{:S(2)}) async-start(), calls=%async_computation.5 | async-start | bytes 4718592 | tf_op jit(solution)/shard_map/all_gather | solution.py:323
  130.7 17.7 %collective-permute-start = (bf16[512,512]{1,0:T(8,128)(2,1)}, bf16[512,512]{1,0:T(8,128)(2,1)S(1)}, u32[]{:S(2)}, u32[]{:S(2)}) collective-permute-start(bf16[512,512]{1,0:T(8,128)(2,1)} %slice.91), channel_id=1, source_target_pairs={{0,1},{1,2},{2,3},{3,4},{4,5},{5,6},{6,7},{7,0},{8,9},{9,10},{10,1... | collective-permute-start | bytes 1572872 | tf_op jit(solution)/shard_map/ppermute | solution.py:143
  130.7 20.1 %collective-permute-start.1 = (bf16[512,512]{1,0:T(8,128)(2,1)}, bf16[512,512]{1,0:T(8,128)(2,1)S(1)}, u32[]{:S(2)}, u32[]{:S(2)}) collective-permute-start(bf16[512,512]{1,0:T(8,128)(2,1)} %slice.91), channel_id=1, source_target_pairs={{0,7},{1,0},{2,1},{3,2},{4,3},{5,4},{6,5},{7,6},{8,15},{9,8},{10,9... | collective-permute-start | bytes 1572872 | tf_op jit(solution)/shard_map/ppermute | solution.py:148
  148.3 25.0 %collective-permute-start.2 = (bf16[512,512]{1,0:T(8,128)(2,1)S(1)}, bf16[512,512]{1,0:T(8,128)(2,1)S(1)}, u32[]{:S(2)}, u32[]{:S(2)}) collective-permute-start(bf16[512,512]{1,0:T(8,128)(2,1)S(1)} %collective-permute-done), channel_id=1, source_target_pairs={{0,1},{1,2},{2,3},{3,4},{4,5},{5,6},{6,7},{7,0},{8,9},{9,10},{10,1... | collective-permute-start | bytes 1572872 | tf_op jit(solution)/shard_map/ppermute | solution.py:143
  150.8 50.2 %copy-start.21 = (bf16[512,512]{1,0:T(8,128)(2,1)}, bf16[512,512]{1,0:T(8,128)(2,1)S(1)}, u32[]{:S(2)}) copy-start(bf16[512,512]{1,0:T(8,128)(2,1)S(1)} %collective-permute-done.1) | copy-start | bytes 1572868
  150.8 25.1 %collective-permute-start.3 = (bf16[512,512]{1,0:T(8,128)(2,1)S(1)}, bf16[512,512]{1,0:T(8,128)(2,1)}, u32[]{:S(2)}, u32[]{:S(2)}) collective-permute-start(bf16[512,512]{1,0:T(8,128)(2,1)S(1)} %collective-permute-done.1), channel_id=1, source_target_pairs={{0,7},{1,0},{2,1},{3,2},{4,3},{5,4},{6,5},{7,6},{8,15},{9,8},{10,9... | collective-permute-start | bytes 1572872 | tf_op jit(solution)/shard_map/ppermute | solution.py:148
  173.3 116.2 %copy-start.23 = (bf16[512,512]{1,0:T(8,128)(2,1)}, bf16[512,512]{1,0:T(8,128)(2,1)S(1)}, u32[]{:S(2)}) copy-start(bf16[512,512]{1,0:T(8,128)(2,1)S(1)} %collective-permute-done.2) | copy-start | bytes 1572868
  173.3 27.7 %collective-permute-start.4 = (bf16[512,512]{1,0:T(8,128)(2,1)S(1)}, bf16[512,512]{1,0:T(8,128)(2,1)}, u32[]{:S(2)}, u32[]{:S(2)}) collective-permute-start(bf16[512,512]{1,0:T(8,128)(2,1)S(1)} %collective-permute-done.2), channel_id=1, source_target_pairs={{0,1},{1,2},{2,3},{3,4},{4,5},{5,6},{6,7},{7,0},{8,9},{9,10},{10,1... | collective-permute-start | bytes 1572872 | tf_op jit(solution)/shard_map/ppermute | solution.py:143
  175.8 685.1 %all-gather.21.cloned.1.call-start = ((), (), s32[]{:S(2)}) async-start(), calls=%async_computation.6 | async-start | bytes 4718592 | tf_op jit(solution)/shard_map/all_gather | solution.py:324
  175.9 130.2 %collective-permute-start.5 = (bf16[512,512]{1,0:T(8,128)(2,1)}, bf16[512,512]{1,0:T(8,128)(2,1)}, u32[]{:S(2)}, u32[]{:S(2)}) collective-permute-start(bf16[512,512]{1,0:T(8,128)(2,1)} %collective-permute-done.3), channel_id=1, source_target_pairs={{0,7},{1,0},{2,1},{3,2},{4,3},{5,4},{6,5},{7,6},{8,15},{9,8},{10,9... | collective-permute-start | bytes 1572872 | tf_op jit(solution)/shard_map/ppermute | solution.py:148
  201.0 105.1 %collective-permute-start.6 = (bf16[512,512]{1,0:T(8,128)(2,1)}, bf16[512,512]{1,0:T(8,128)(2,1)}, u32[]{:S(2)}, u32[]{:S(2)}) collective-permute-start(bf16[512,512]{1,0:T(8,128)(2,1)} %collective-permute-done.4), channel_id=1, source_target_pairs={{0,1},{1,2},{2,3},{3,4},{4,5},{5,6},{6,7},{7,0},{8,9},{9,10},{10,1... | collective-permute-start | bytes 1572872 | tf_op jit(solution)/shard_map/ppermute | solution.py:143
  300.5 5.7 copy-start.4
  300.5 5.7 copy-start.22
  356.7 5.6 copy-start
  372.0 5.6 copy-start
  402.6 5.7 copy-start
  585.4 11.6 copy-start.13
  585.5 11.6 copy-start.19
  609.9 7.4 copy-start.32
  614.3 791.9 %all-reduce.11.cloned.1.call-start = ((), (), s32[]{:S(2)}) async-start(), calls=%async_computation.7 | async-start | bytes 25165824
  861.0 12.1 copy-start.5
  1179.4 5.6 copy-start.31
  1179.4 5.7 copy-start.29
  (43 other events, 173.9 us)
Sparse Core Ops, SparseCore 0:
  10.9 57.8 all-gather.8
  71.7 55.3 all-gather.12
  130.2 75.1 all-gather.14
  207.3 78.8 all-gather.10
  288.8 72.7 all-gather.16
  363.5 71.6 all-gather.18
  614.4 74.3 all-gather.20
  1174.1 232.0 all-reduce.10
